TPU v7x, 256 devices: a whole 4x4x8 slice. The times are simulated.
256 devices in a mesh: gx: 4 (over x), gy: 8 (over z), gz: 8 (over y, core).
Axes of the slice: x: 4, y: 4, z: 8, core: 2. Of those that a mesh axis runs over, the one named last changes fastest.
Arguments:
- solution_old: float32 [1024, 32, 1024], P(('gx', 'gy', 'gz')), may hold values from -6 to 6
- right_side: float32 [1024, 32, 1024], P(('gx', 'gy', 'gz')), may hold values from -6 to 6
- acoef: float32 [1024, 32, 1024], P(('gx', 'gy', 'gz')), may hold values from 0.05 to 1
- bcoef: float32 [1024, 32, 1024], P(('gx', 'gy', 'gz')), may hold values from 0.25 to 4
- corners: int32 [3, 1024], replicated, may hold values from 0 to 992, as said below
Outputs:
- solution: float32 [128, 256, 1024], P('gx', 'gy', 'gz')
- residual: float32 [128, 256, 1024], P('gx', 'gy', 'gz')
Inputs may be any that keep to these rules, and one draw needn't show every extreme that they name: `corners`: each corner is a multiple of 32 in every dimension and the boxes tile the level one to one. The new owner of a box, the device whose block of 32 x 32 x 128 cells holds its corner, has the same gx and gz indices as the device that holds its row. At most one box moves from one device to any other device, and at most min(3, 7) boxes leave or reach one device; in each group of devices with one gx and one gz index, one device swaps a box with each of that many others, and every other device of the group passes one box on along a cycle through them.
All inputs are finite; a program needn't handle non-finite values.
Results may differ from a plain program's by a relative error of at most 0.00002.
Values sent between devices are 32-bit elements; how exact they have to be, the bound alone decides.
No kernel may reach another device: no remote copies, remote signals or barrier semaphores. Data moves between devices by JAX's collectives and lax.ppermute only.
A program may use at most 64 MiB of HBM per device.

v0:
```python
import jax
import jax.numpy as jnp
from jax import lax
from jax.sharding import PartitionSpec as P

BXB = 1
BYB = 1
BZB = 4
SWEEPS = 2


def extended(block, sides, width):
    for axis, dim in sides:
        count = lax.axis_size(axis)
        forward = [(i, i + 1) for i in range(count - 1)]
        backward = [(target, source) for source, target in forward]
        low = lax.ppermute(
            lax.slice_in_dim(block, block.shape[dim] - width, None, axis=dim), axis, forward
        )
        high = lax.ppermute(lax.slice_in_dim(block, 0, width, axis=dim), axis, backward)
        block = jnp.concatenate([low, block, high], axis=dim)
    return block


def face_coefs(padded):
    face_x = 0.5 * (padded[1:, 1:-1, 1:-1] + padded[:-1, 1:-1, 1:-1])
    face_y = 0.5 * (padded[1:-1, 1:, 1:-1] + padded[1:-1, :-1, 1:-1])
    face_z = 0.5 * (padded[1:-1, 1:-1, 1:] + padded[1:-1, 1:-1, :-1])
    return (face_x, face_y, face_z)


def diag_of(absorb, face_set):
    face_x, face_y, face_z = face_set
    return (
        absorb
        + (face_x[1:] + face_x[:-1])
        + (face_y[:, 1:] + face_y[:, :-1])
        + (face_z[:, :, 1:] + face_z[:, :, :-1])
    )


def neighbors(padded, face_set):
    face_x, face_y, face_z = face_set
    summed = face_x[1:] * padded[2:, 1:-1, 1:-1] + face_x[:-1] * padded[:-2, 1:-1, 1:-1]
    summed = (
        summed + face_y[:, 1:] * padded[1:-1, 2:, 1:-1] + face_y[:, :-1] * padded[1:-1, :-2, 1:-1]
    )
    summed = (
        summed
        + face_z[:, :, 1:] * padded[1:-1, 1:-1, 2:]
        + face_z[:, :, :-1] * padded[1:-1, 1:-1, :-2]
    )
    return summed


def checker(grid_shape):
    return (
        lax.broadcasted_iota(jnp.int32, grid_shape, 0)
        + lax.broadcasted_iota(jnp.int32, grid_shape, 1)
        + lax.broadcasted_iota(jnp.int32, grid_shape, 2)
    ) % 2


def solution_faces(field):
    return extended(field, (("gx", 0), ("gy", 1), ("gz", 2)), 1)


def to_block(boxes, source):
    box_edge = boxes.shape[1]
    picked = jnp.take(boxes, source, axis=0)
    grouped = picked.reshape(BXB, BYB, BZB, box_edge, box_edge, box_edge)
    return grouped.transpose(0, 3, 1, 4, 2, 5).reshape(
        BXB * box_edge, BYB * box_edge, BZB * box_edge
    )


def pack_sent(field_box, send_index, send_live):
    return jnp.take(field_box, send_index, axis=0) * send_live[:, None, None]


def per_device(solution_old, right_side, acoef, bcoef, corners):
    box_edge = solution_old.shape[1]
    per_dev = solution_old.shape[0]
    span_x = BXB * box_edge
    span_y = BYB * box_edge
    span_z = BZB * box_edge
    width_x = lax.axis_size("gx")
    width_y = lax.axis_size("gy")
    width_z = lax.axis_size("gz")
    myself = lax.axis_index("gy")
    table = corners.reshape(3, width_x, width_y, width_z, per_dev)
    mine_x = lax.dynamic_index_in_dim(table, lax.axis_index("gx"), 1, keepdims=False)
    mine_z = lax.dynamic_index_in_dim(mine_x, lax.axis_index("gz"), 2, keepdims=False)
    corner_x, corner_y, corner_z = (mine_z[0], mine_z[1], mine_z[2])
    owner_grid = corner_y // span_y
    inner_grid = (
        corner_x % span_x // box_edge * BYB + corner_y % span_y // box_edge
    ) * BZB + corner_z % span_z // box_edge
    my_owner = lax.dynamic_index_in_dim(owner_grid, myself, 0, keepdims=False)
    my_inner = lax.dynamic_index_in_dim(inner_grid, myself, 0, keepdims=False)
    peer_ids = jnp.arange(width_y, dtype=jnp.int32)
    slot_ids = jnp.arange(per_dev, dtype=jnp.int32)
    outgoing = (my_owner[None, :] == peer_ids[:, None]) & (peer_ids[:, None] != myself)
    send_index = jnp.sum(jnp.where(outgoing, slot_ids[None, :], 0), axis=1)
    send_live = jnp.any(outgoing, axis=1).astype(jnp.float32)
    sol_sent = pack_sent(solution_old, send_index, send_live)
    rhs_sent = pack_sent(right_side, send_index, send_live)
    absorb_sent = pack_sent(acoef, send_index, send_live)
    diffuse_sent = pack_sent(bcoef, send_index, send_live)
    sol_got, rhs_got, absorb_got, diffuse_got = (
        lax.all_to_all(sol_sent, "gy", split_axis=0, concat_axis=0, tiled=True),
        lax.all_to_all(rhs_sent, "gy", split_axis=0, concat_axis=0, tiled=True),
        lax.all_to_all(absorb_sent, "gy", split_axis=0, concat_axis=0, tiled=True),
        lax.all_to_all(diffuse_sent, "gy", split_axis=0, concat_axis=0, tiled=True),
    )
    incoming = (owner_grid == myself) & (peer_ids[:, None] != myself)
    recv_inner = jnp.sum(jnp.where(incoming, inner_grid, 0), axis=1)
    recv_live = jnp.any(incoming, axis=1)
    cand_inner = jnp.concatenate(
        [jnp.where(my_owner == myself, my_inner, -1), jnp.where(recv_live, recv_inner, -1)]
    )
    cand_ids = jnp.arange(per_dev + width_y, dtype=jnp.int32)
    source = jnp.sum(
        jnp.where(cand_inner[None, :] == slot_ids[:, None], cand_ids[None, :], 0), axis=1
    )
    solution = to_block(jnp.concatenate([solution_old, sol_got]), source)
    forcing = to_block(jnp.concatenate([right_side, rhs_got]), source)
    absorb = to_block(jnp.concatenate([acoef, absorb_got]), source)
    diffuse = to_block(jnp.concatenate([bcoef, diffuse_got]), source)
    diffuse_padded = extended(diffuse, (("gx", 0), ("gy", 1), ("gz", 2)), 1)
    face_set = face_coefs(diffuse_padded)
    diagonal = diag_of(absorb, face_set)
    parity = checker(solution.shape)
    for sweep_no in range(SWEEPS):
        for colour in (0, 1):
            padded = solution_faces(solution)
            updated = (forcing + neighbors(padded, face_set)) / diagonal
            solution = jnp.where(parity == colour, updated, solution)
    residual = forcing - (diagonal * solution - neighbors(solution_faces(solution), face_set))
    return (solution, residual)


def solution(mesh):
    in_specs = (
        P(("gx", "gy", "gz"), None, None),
        P(("gx", "gy", "gz"), None, None),
        P(("gx", "gy", "gz"), None, None),
        P(("gx", "gy", "gz"), None, None),
        P(),
    )
    out_specs = (P("gx", "gy", "gz"), P("gx", "gy", "gz"))
    return jax.shard_map(
        per_device, mesh=mesh, in_specs=in_specs, out_specs=out_specs, check_vma=False
    )
```

profile of v0, /device:TPU:1, one launch (start us, length us, event | category | flops | bytes accessed | tf_op | source)
XLA Modules:
  0.0 355.2 jit_solution(902741867258370207)
XLA Ops:
  12.5 36.1 %all_to_all.20 = f32[8,32,1024]{2,1,0:T(8,128)} all-to-all(f32[8,32,1024]{2,1,0:T(8,128)S(1)} %get-tuple-element.55), channel_id=1, replica_groups=mesh['gx'=4,'gy'=8,'gz'=8] {'gy'}, dimensions={0} | all-to-all | bytes 2097152 | tf_op jit(solution)/shard_map/all_to_all | solution.py:114
  48.6 28.8 %all_to_all.21 = f32[8,32,1024]{2,1,0:T(8,128)} all-to-all(f32[8,32,1024]{2,1,0:T(8,128)S(1)} %get-tuple-element.56), channel_id=1, replica_groups=mesh['gx'=4,'gy'=8,'gz'=8] {'gy'}, dimensions={0} | all-to-all | bytes 2097152 | tf_op jit(solution)/shard_map/all_to_all | solution.py:111
  77.4 27.3 %all_to_all.22 = f32[8,32,1024]{2,1,0:T(8,128)} all-to-all(f32[8,32,1024]{2,1,0:T(8,128)S(1)} %get-tuple-element.57), channel_id=1, replica_groups=mesh['gx'=4,'gy'=8,'gz'=8] {'gy'}, dimensions={0} | all-to-all | bytes 2097152 | tf_op jit(solution)/shard_map/all_to_all | solution.py:113
  104.7 3.7 %all-to-all-start = ((f32[8,32,1024]{2,1,0:T(8,128)}), f32[8,32,1024]{2,1,0:T(8,128)S(1)}, u32[]{:S(2)}, u32[]{:S(2)}) async-start(f32[8,32,1024]{2,1,0:T(8,128)} %get-tuple-element.58), calls=%async_computation | async-start | bytes 2097152 | tf_op jit(solution)/shard_map/all_to_all | solution.py:112
  123.5 10.0 %all-to-all-done = f32[8,32,1024]{2,1,0:T(8,128)S(1)} async-done(((f32[8,32,1024]{2,1,0:T(8,128)}), f32[8,32,1024]{2,1,0:T(8,128)S(1)}, u32[]{:S(2)}, u32[]{:S(2)}) %all-to-all-start) | async-done | bytes 1048608 | tf_op jit(solution)/shard_map/all_to_all | solution.py:112
  148.5 4.7 %copy.375 = f32[1,1,4,32,32,32]{5,2,4,1,3,0:T(4,128)} copy(f32[1,1,4,32,32,32]{5,4,3,2,1,0:T(8,128)} %reshape.65) | data formatting | bytes 1048576 | tf_op jit(solution)/shard_map/reshape | solution.py:71
  172.9 4.0 %collective-permute-start.1 = (f32[1,32,128]{2,1,0:T(8,128)S(1)}, f32[1,32,128]{2,1,0:T(8,128)S(1)}, u32[]{:S(2)}, u32[]{:S(2)}) collective-permute-start(f32[1,32,128]{2,1,0:T(8,128)S(1)} %slice.326), channel_id=1, source_target_pairs={{0,64},{64,128},{128,192},{1,65},{65,129},{129,193},{2,66},{66,130... | collective-permute-start | bytes 49160 | tf_op jit(solution)/shard_map/ppermute | solution.py:17
  179.9 4.0 %collective-permute-start.7 = (f32[34,1,128]{2,0,1:T(8,128)S(1)}, f32[34,1,128]{2,0,1:T(8,128)S(1)}, u32[]{:S(2)}, u32[]{:S(2)}) collective-permute-start(f32[34,1,128]{2,0,1:T(8,128)S(1)} %copy.312), channel_id=1, source_target_pairs={{0,8},{8,16},{16,24},{24,32},{32,40},{40,48},{48,56},{1,9},{9,17},... | collective-permute-start | bytes 52232 | tf_op jit(solution)/shard_map/ppermute | solution.py:17
  185.4 4.0 %collective-permute-start.5 = (f32[34,1,128]{2,0,1:T(8,128)S(1)}, f32[34,1,128]{2,0,1:T(8,128)S(1)}, u32[]{:S(2)}, u32[]{:S(2)}) collective-permute-start(f32[34,1,128]{2,0,1:T(8,128)S(1)} %copy.368), channel_id=1, source_target_pairs={{0,8},{8,16},{16,24},{24,32},{32,40},{40,48},{48,56},{1,9},{9,17},... | collective-permute-start | bytes 52232 | tf_op jit(solution)/shard_map/ppermute | solution.py:17
  193.9 9.7 %collective-permute-start.9 = (f32[34,34,1]{1,0,2:T(8,128)S(1)}, f32[34,34,1]{1,0,2:T(8,128)S(1)}, u32[]{:S(2)}, u32[]{:S(2)}) collective-permute-start(f32[34,34,1]{1,0,2:T(8,128)S(1)} %copy.318), channel_id=1, source_target_pairs={{0,1},{1,2},{2,3},{3,4},{4,5},{5,6},{6,7},{8,9},{9,10},{10,11},{11... | collective-permute-start | bytes 13880 | tf_op jit(solution)/shard_map/ppermute | solution.py:17
  208.5 3.6 %collective-permute-start.11 = (f32[34,34,1]{1,0,2:T(8,128)S(1)}, f32[34,34,1]{1,0,2:T(8,128)S(1)}, u32[]{:S(2)}, u32[]{:S(2)}) collective-permute-start(f32[34,34,1]{1,0,2:T(8,128)S(1)} %copy.324), channel_id=1, source_target_pairs={{0,1},{1,2},{2,3},{3,4},{4,5},{5,6},{6,7},{8,9},{9,10},{10,11},{11... | collective-permute-start | bytes 13880 | tf_op jit(solution)/shard_map/ppermute | solution.py:17
  227.3 4.9 %collective-permute-start.13 = (f32[1,32,128]{2,1,0:T(8,128)S(1)}, f32[1,32,128]{2,1,0:T(8,128)S(1)}, u32[]{:S(2)}, u32[]{:S(2)}) collective-permute-start(f32[1,32,128]{2,1,0:T(8,128)S(1)} %get-tuple-element.50), channel_id=1, source_target_pairs={{0,64},{64,128},{128,192},{1,65},{65,129},{129,193},{2,66},{66,130... | collective-permute-start | bytes 49160 | tf_op jit(solution)/shard_map/ppermute | solution.py:17
  234.4 4.4 %collective-permute-start.15 = (f32[34,1,128]{2,0,1:T(8,128)S(1)}, f32[34,1,128]{2,0,1:T(8,128)S(1)}, u32[]{:S(2)}, u32[]{:S(2)}) collective-permute-start(f32[34,1,128]{2,0,1:T(8,128)S(1)} %copy.329), channel_id=1, source_target_pairs={{0,8},{8,16},{16,24},{24,32},{32,40},{40,48},{48,56},{1,9},{9,17},... | collective-permute-start | bytes 52232 | tf_op jit(solution)/shard_map/ppermute | solution.py:17
  242.6 5.3 %collective-permute-start.17 = (f32[34,34,1]{1,0,2:T(8,128)S(1)}, f32[34,34,1]{1,0,2:T(8,128)S(1)}, u32[]{:S(2)}, u32[]{:S(2)}) collective-permute-start(f32[34,34,1]{1,0,2:T(8,128)S(1)} %copy.335), channel_id=1, source_target_pairs={{0,1},{1,2},{2,3},{3,4},{4,5},{5,6},{6,7},{8,9},{9,10},{10,11},{11... | collective-permute-start | bytes 13880 | tf_op jit(solution)/shard_map/ppermute | solution.py:17
  255.7 3.7 %fusion.51 = f32[32,32,128]{2,1,0:T(8,128)S(1)} fusion(f32[32,32,128]{2,1,0:T(8,128)} %copy-done.3, f32[32,32,128]{2,1,0:T(8,128)S(1)} %reshape.64, f32[34,34,1]{2,1,0:T(8,128)} %copy.336, f32[34,1,128]{2,1,0:T(1,128)S(1)} %copy.328, f32[34,1,128]{2,1,0:T(1,128)S(1)} %copy.330, f32[1,32,128]{2,1,0:T(8,128)S(1)} %collective-permute-done.12, ...), kind=kLoop, calls=%fused_computation.144 | loop fusion | flops 6815744 | bytes 5319712 | tf_op jit(solution)/shard_map/jit(_where)/select_n | solution.py:138
  260.8 4.5 %collective-permute-start.19 = (f32[1,32,128]{2,1,0:T(8,128)S(1)}, f32[1,32,128]{2,1,0:T(8,128)S(1)}, u32[]{:S(2)}, u32[]{:S(2)}) collective-permute-start(f32[1,32,128]{2,1,0:T(8,128)S(1)} %get-tuple-element.48), channel_id=1, source_target_pairs={{0,64},{64,128},{128,192},{1,65},{65,129},{129,193},{2,66},{66,130... | collective-permute-start | bytes 49160 | tf_op jit(solution)/shard_map/ppermute | solution.py:17
  267.5 4.6 %collective-permute-start.21 = (f32[34,1,128]{2,0,1:T(8,128)S(1)}, f32[34,1,128]{2,0,1:T(8,128)S(1)}, u32[]{:S(2)}, u32[]{:S(2)}) collective-permute-start(f32[34,1,128]{2,0,1:T(8,128)S(1)} %copy.339), channel_id=1, source_target_pairs={{0,8},{8,16},{16,24},{24,32},{32,40},{40,48},{48,56},{1,9},{9,17},... | collective-permute-start | bytes 52232 | tf_op jit(solution)/shard_map/ppermute | solution.py:17
  287.3 3.7 %fusion.37 = f32[32,32,128]{2,1,0:T(8,128)S(1)} fusion(f32[32,32,128]{2,1,0:T(8,128)} %copy-done.1, f32[32,32,128]{2,1,0:T(8,128)S(1)} %reshape.64, f32[34,34,1]{2,1,0:T(8,128)} %copy.346, f32[34,1,128]{2,1,0:T(1,128)S(1)} %copy.338, f32[34,1,128]{2,1,0:T(1,128)S(1)} %copy.340, f32[1,32,128]{2,1,0:T(8,128)S(1)} %collective-permute-done.18, ...), kind=kLoop, calls=%fused_computation.112 | loop fusion | flops 6815744 | bytes 5319712 | tf_op jit(solution)/shard_map/jit(_where)/select_n | solution.py:138
  292.3 4.5 %collective-permute-start.25 = (f32[1,32,128]{2,1,0:T(8,128)S(1)}, f32[1,32,128]{2,1,0:T(8,128)S(1)}, u32[]{:S(2)}, u32[]{:S(2)}) collective-permute-start(f32[1,32,128]{2,1,0:T(8,128)S(1)} %get-tuple-element.46), channel_id=1, source_target_pairs={{0,64},{64,128},{128,192},{1,65},{65,129},{129,193},{2,66},{66,130... | collective-permute-start | bytes 49160 | tf_op jit(solution)/shard_map/ppermute | solution.py:17
  299.1 4.6 %collective-permute-start.27 = (f32[34,1,128]{2,0,1:T(8,128)S(1)}, f32[34,1,128]{2,0,1:T(8,128)S(1)}, u32[]{:S(2)}, u32[]{:S(2)}) collective-permute-start(f32[34,1,128]{2,0,1:T(8,128)S(1)} %copy.349), channel_id=1, source_target_pairs={{0,8},{8,16},{16,24},{24,32},{32,40},{40,48},{48,56},{1,9},{9,17},... | collective-permute-start | bytes 52232 | tf_op jit(solution)/shard_map/ppermute | solution.py:17
  318.9 3.7 %fusion.23 = f32[32,32,128]{2,1,0:T(8,128)S(1)} fusion(f32[32,32,128]{2,1,0:T(8,128)} %copy-done.2, f32[32,32,128]{2,1,0:T(8,128)S(1)} %reshape.64, f32[34,34,1]{2,1,0:T(8,128)} %copy.356, f32[34,1,128]{2,1,0:T(1,128)S(1)} %copy.348, f32[34,1,128]{2,1,0:T(1,128)S(1)} %copy.350, f32[1,32,128]{2,1,0:T(8,128)S(1)} %collective-permute-done.24, ...), kind=kLoop, calls=%fused_computation.80 | loop fusion | flops 6815744 | bytes 5319712 | tf_op jit(solution)/shard_map/jit(_where)/select_n | solution.py:138
  323.9 4.5 %collective-permute-start.31 = (f32[1,32,128]{2,1,0:T(8,128)S(1)}, f32[1,32,128]{2,1,0:T(8,128)S(1)}, u32[]{:S(2)}, u32[]{:S(2)}) collective-permute-start(f32[1,32,128]{2,1,0:T(8,128)S(1)} %get-tuple-element.44), channel_id=1, source_target_pairs={{0,64},{64,128},{128,192},{1,65},{65,129},{129,193},{2,66},{66,130... | collective-permute-start | bytes 49160 | tf_op jit(solution)/shard_map/ppermute | solution.py:17
  330.6 4.6 %collective-permute-start.33 = (f32[34,1,128]{2,0,1:T(8,128)S(1)}, f32[34,1,128]{2,0,1:T(8,128)S(1)}, u32[]{:S(2)}, u32[]{:S(2)}) collective-permute-start(f32[34,1,128]{2,0,1:T(8,128)S(1)} %copy.359), channel_id=1, source_target_pairs={{0,8},{8,16},{16,24},{24,32},{32,40},{40,48},{48,56},{1,9},{9,17},... | collective-permute-start | bytes 52232 | tf_op jit(solution)/shard_map/ppermute | solution.py:17
  350.4 4.8 %fusion.9 = f32[32,32,128]{2,1,0:T(8,128)} fusion(f32[32,32,128]{2,1,0:T(8,128)S(1)} %reshape.64, f32[34,34,1]{2,1,0:T(8,128)} %copy.366, f32[34,1,128]{2,1,0:T(1,128)S(1)} %copy.358, f32[34,1,128]{2,1,0:T(1,128)S(1)} %copy.360, f32[1,32,128]{2,1,0:T(8,128)S(1)} %collective-permute-done.30, f32[32,32,128]{2,1,0:T(8,128)} %copy-done, ...), kind=kLoop, calls=%fused_computation.48 | loop fusion | flops 4980736 | bytes 5319712 | tf_op jit(solution)/shard_map/sub | solution.py:139
  (217 shorter events, 159.8 us)
Async XLA Ops:
  104.7 28.7 %all-to-all-start = ((f32[8,32,1024]{2,1,0:T(8,128)}), f32[8,32,1024]{2,1,0:T(8,128)S(1)}, u32[]{:S(2)}, u32[]{:S(2)}) async-start(f32[8,32,1024]{2,1,0:T(8,128)} %get-tuple-element.58), calls=%async_computation | async-start | bytes 2097152 | tf_op jit(solution)/shard_map/all_to_all | solution.py:112
  142.2 36.2 %collective-permute-start.3 = (f32[1,32,128]{2,1,0:T(8,128)S(1)}, f32[1,32,128]{2,1,0:T(8,128)S(1)}, u32[]{:S(2)}, u32[]{:S(2)}) collective-permute-start(f32[1,32,128]{2,1,0:T(8,128)S(1)} %slice.333), channel_id=1, source_target_pairs={{0,64},{64,128},{128,192},{1,65},{65,129},{129,193},{2,66},{66,130... | collective-permute-start | bytes 49160 | tf_op jit(solution)/shard_map/ppermute | solution.py:17
  165.1 13.4 %collective-permute-start.2 = (f32[1,32,128]{2,1,0:T(8,128)S(1)}, f32[1,32,128]{2,1,0:T(8,128)S(1)}, u32[]{:S(2)}, u32[]{:S(2)}) collective-permute-start(f32[1,32,128]{2,1,0:T(8,128)S(1)} %slice.329), channel_id=1, source_target_pairs={{64,0},{128,64},{192,128},{65,1},{129,65},{193,129},{66,2},{130,66... | collective-permute-start | bytes 49160 | tf_op jit(solution)/shard_map/ppermute | solution.py:20
  172.9 11.1 %collective-permute-start.1 = (f32[1,32,128]{2,1,0:T(8,128)S(1)}, f32[1,32,128]{2,1,0:T(8,128)S(1)}, u32[]{:S(2)}, u32[]{:S(2)}) collective-permute-start(f32[1,32,128]{2,1,0:T(8,128)S(1)} %slice.326), channel_id=1, source_target_pairs={{0,64},{64,128},{128,192},{1,65},{65,129},{129,193},{2,66},{66,130... | collective-permute-start | bytes 49160 | tf_op jit(solution)/shard_map/ppermute | solution.py:17
  177.0 7.1 %collective-permute-start = (f32[1,32,128]{2,1,0:T(8,128)S(1)}, f32[1,32,128]{2,1,0:T(8,128)S(1)}, u32[]{:S(2)}, u32[]{:S(2)}) collective-permute-start(f32[1,32,128]{2,1,0:T(8,128)S(1)} %slice.324), channel_id=1, source_target_pairs={{64,0},{128,64},{192,128},{65,1},{129,65},{193,129},{66,2},{130,66... | collective-permute-start | bytes 49160 | tf_op jit(solution)/shard_map/ppermute | solution.py:20
  178.6 10.8 %collective-permute-start.6 = (f32[34,1,128]{2,0,1:T(8,128)S(1)}, f32[34,1,128]{2,0,1:T(8,128)S(1)}, u32[]{:S(2)}, u32[]{:S(2)}) collective-permute-start(f32[34,1,128]{2,0,1:T(8,128)S(1)} %copy.310), channel_id=1, source_target_pairs={{8,0},{16,8},{24,16},{32,24},{40,32},{48,40},{56,48},{9,1},{17,9},... | collective-permute-start | bytes 52232 | tf_op jit(solution)/shard_map/ppermute | solution.py:20
  179.9 9.6 %collective-permute-start.7 = (f32[34,1,128]{2,0,1:T(8,128)S(1)}, f32[34,1,128]{2,0,1:T(8,128)S(1)}, u32[]{:S(2)}, u32[]{:S(2)}) collective-permute-start(f32[34,1,128]{2,0,1:T(8,128)S(1)} %copy.312), channel_id=1, source_target_pairs={{0,8},{8,16},{16,24},{24,32},{32,40},{40,48},{48,56},{1,9},{9,17},... | collective-permute-start | bytes 52232 | tf_op jit(solution)/shard_map/ppermute | solution.py:17
  184.1 6.9 %collective-permute-start.4 = (f32[34,1,128]{2,0,1:T(8,128)S(1)}, f32[34,1,128]{2,0,1:T(8,128)S(1)}, u32[]{:S(2)}, u32[]{:S(2)}) collective-permute-start(f32[34,1,128]{2,0,1:T(8,128)S(1)} %copy.367), channel_id=1, source_target_pairs={{8,0},{16,8},{24,16},{32,24},{40,32},{48,40},{56,48},{9,1},{17,9},... | collective-permute-start | bytes 52232 | tf_op jit(solution)/shard_map/ppermute | solution.py:20
  193.9 21.7 %collective-permute-start.9 = (f32[34,34,1]{1,0,2:T(8,128)S(1)}, f32[34,34,1]{1,0,2:T(8,128)S(1)}, u32[]{:S(2)}, u32[]{:S(2)}) collective-permute-start(f32[34,34,1]{1,0,2:T(8,128)S(1)} %copy.318), channel_id=1, source_target_pairs={{0,1},{1,2},{2,3},{3,4},{4,5},{5,6},{6,7},{8,9},{9,10},{10,11},{11... | collective-permute-start | bytes 13880 | tf_op jit(solution)/shard_map/ppermute | solution.py:17
  205.0 11.8 %collective-permute-start.8 = (f32[34,34,1]{1,0,2:T(8,128)S(1)}, f32[34,34,1]{1,0,2:T(8,128)S(1)}, u32[]{:S(2)}, u32[]{:S(2)}) collective-permute-start(f32[34,34,1]{1,0,2:T(8,128)S(1)} %copy.316), channel_id=1, source_target_pairs={{1,0},{2,1},{3,2},{4,3},{5,4},{6,5},{7,6},{9,8},{10,9},{11,10},{12... | collective-permute-start | bytes 13880 | tf_op jit(solution)/shard_map/ppermute | solution.py:20
  208.5 11.5 %collective-permute-start.11 = (f32[34,34,1]{1,0,2:T(8,128)S(1)}, f32[34,34,1]{1,0,2:T(8,128)S(1)}, u32[]{:S(2)}, u32[]{:S(2)}) collective-permute-start(f32[34,34,1]{1,0,2:T(8,128)S(1)} %copy.324), channel_id=1, source_target_pairs={{0,1},{1,2},{2,3},{3,4},{4,5},{5,6},{6,7},{8,9},{9,10},{10,11},{11... | collective-permute-start | bytes 13880 | tf_op jit(solution)/shard_map/ppermute | solution.py:17
  213.6 7.6 %collective-permute-start.10 = (f32[34,34,1]{1,0,2:T(8,128)S(1)}, f32[34,34,1]{1,0,2:T(8,128)S(1)}, u32[]{:S(2)}, u32[]{:S(2)}) collective-permute-start(f32[34,34,1]{1,0,2:T(8,128)S(1)} %copy.322), channel_id=1, source_target_pairs={{1,0},{2,1},{3,2},{4,3},{5,4},{6,5},{7,6},{9,8},{10,9},{11,10},{12... | collective-permute-start | bytes 13880 | tf_op jit(solution)/shard_map/ppermute | solution.py:20
  226.0 6.2 %collective-permute-start.12 = (f32[1,32,128]{2,1,0:T(8,128)S(1)}, f32[1,32,128]{2,1,0:T(8,128)S(1)}, u32[]{:S(2)}, u32[]{:S(2)}) collective-permute-start(f32[1,32,128]{2,1,0:T(8,128)S(1)} %get-tuple-element.51), channel_id=1, source_target_pairs={{64,0},{128,64},{192,128},{65,1},{129,65},{193,129},{66,2},{130,66... | collective-permute-start | bytes 49160 | tf_op jit(solution)/shard_map/ppermute | solution.py:20
  227.3 5.8 %collective-permute-start.13 = (f32[1,32,128]{2,1,0:T(8,128)S(1)}, f32[1,32,128]{2,1,0:T(8,128)S(1)}, u32[]{:S(2)}, u32[]{:S(2)}) collective-permute-start(f32[1,32,128]{2,1,0:T(8,128)S(1)} %get-tuple-element.50), channel_id=1, source_target_pairs={{0,64},{64,128},{128,192},{1,65},{65,129},{129,193},{2,66},{66,130... | collective-permute-start | bytes 49160 | tf_op jit(solution)/shard_map/ppermute | solution.py:17
  242.6 8.7 %collective-permute-start.17 = (f32[34,34,1]{1,0,2:T(8,128)S(1)}, f32[34,34,1]{1,0,2:T(8,128)S(1)}, u32[]{:S(2)}, u32[]{:S(2)}) collective-permute-start(f32[34,34,1]{1,0,2:T(8,128)S(1)} %copy.335), channel_id=1, source_target_pairs={{0,1},{1,2},{2,3},{3,4},{4,5},{5,6},{6,7},{8,9},{9,10},{10,11},{11... | collective-permute-start | bytes 13880 | tf_op jit(solution)/shard_map/ppermute | solution.py:17
  259.5 5.9 %collective-permute-start.18 = (f32[1,32,128]{2,1,0:T(8,128)S(1)}, f32[1,32,128]{2,1,0:T(8,128)S(1)}, u32[]{:S(2)}, u32[]{:S(2)}) collective-permute-start(f32[1,32,128]{2,1,0:T(8,128)S(1)} %get-tuple-element.49), channel_id=1, source_target_pairs={{64,0},{128,64},{192,128},{65,1},{129,65},{193,129},{66,2},{130,66... | collective-permute-start | bytes 49160 | tf_op jit(solution)/shard_map/ppermute | solution.py:20
  266.2 5.9 %collective-permute-start.20 = (f32[34,1,128]{2,0,1:T(8,128)S(1)}, f32[34,1,128]{2,0,1:T(8,128)S(1)}, u32[]{:S(2)}, u32[]{:S(2)}) collective-permute-start(f32[34,1,128]{2,0,1:T(8,128)S(1)} %copy.337), channel_id=1, source_target_pairs={{8,0},{16,8},{24,16},{32,24},{40,32},{48,40},{56,48},{9,1},{17,9},... | collective-permute-start | bytes 52232 | tf_op jit(solution)/shard_map/ppermute | solution.py:20
  275.9 7.0 %collective-permute-start.23 = (f32[34,34,1]{1,0,2:T(8,128)S(1)}, f32[34,34,1]{1,0,2:T(8,128)S(1)}, u32[]{:S(2)}, u32[]{:S(2)}) collective-permute-start(f32[34,34,1]{1,0,2:T(8,128)S(1)} %copy.345), channel_id=1, source_target_pairs={{0,1},{1,2},{2,3},{3,4},{4,5},{5,6},{6,7},{8,9},{9,10},{10,11},{11... | collective-permute-start | bytes 13880 | tf_op jit(solution)/shard_map/ppermute | solution.py:17
  291.0 5.9 %collective-permute-start.24 = (f32[1,32,128]{2,1,0:T(8,128)S(1)}, f32[1,32,128]{2,1,0:T(8,128)S(1)}, u32[]{:S(2)}, u32[]{:S(2)}) collective-permute-start(f32[1,32,128]{2,1,0:T(8,128)S(1)} %get-tuple-element.47), channel_id=1, source_target_pairs={{64,0},{128,64},{192,128},{65,1},{129,65},{193,129},{66,2},{130,66... | collective-permute-start | bytes 49160 | tf_op jit(solution)/shard_map/ppermute | solution.py:20
  297.8 5.9 %collective-permute-start.26 = (f32[34,1,128]{2,0,1:T(8,128)S(1)}, f32[34,1,128]{2,0,1:T(8,128)S(1)}, u32[]{:S(2)}, u32[]{:S(2)}) collective-permute-start(f32[34,1,128]{2,0,1:T(8,128)S(1)} %copy.347), channel_id=1, source_target_pairs={{8,0},{16,8},{24,16},{32,24},{40,32},{48,40},{56,48},{9,1},{17,9},... | collective-permute-start | bytes 52232 | tf_op jit(solution)/shard_map/ppermute | solution.py:20
  307.4 7.0 %collective-permute-start.29 = (f32[34,34,1]{1,0,2:T(8,128)S(1)}, f32[34,34,1]{1,0,2:T(8,128)S(1)}, u32[]{:S(2)}, u32[]{:S(2)}) collective-permute-start(f32[34,34,1]{1,0,2:T(8,128)S(1)} %copy.355), channel_id=1, source_target_pairs={{0,1},{1,2},{2,3},{3,4},{4,5},{5,6},{6,7},{8,9},{9,10},{10,11},{11... | collective-permute-start | bytes 13880 | tf_op jit(solution)/shard_map/ppermute | solution.py:17
  322.6 5.9 %collective-permute-start.30 = (f32[1,32,128]{2,1,0:T(8,128)S(1)}, f32[1,32,128]{2,1,0:T(8,128)S(1)}, u32[]{:S(2)}, u32[]{:S(2)}) collective-permute-start(f32[1,32,128]{2,1,0:T(8,128)S(1)} %get-tuple-element.45), channel_id=1, source_target_pairs={{64,0},{128,64},{192,128},{65,1},{129,65},{193,129},{66,2},{130,66... | collective-permute-start | bytes 49160 | tf_op jit(solution)/shard_map/ppermute | solution.py:20
  329.3 5.9 %collective-permute-start.32 = (f32[34,1,128]{2,0,1:T(8,128)S(1)}, f32[34,1,128]{2,0,1:T(8,128)S(1)}, u32[]{:S(2)}, u32[]{:S(2)}) collective-permute-start(f32[34,1,128]{2,0,1:T(8,128)S(1)} %copy.357), channel_id=1, source_target_pairs={{8,0},{16,8},{24,16},{32,24},{40,32},{48,40},{56,48},{9,1},{17,9},... | collective-permute-start | bytes 52232 | tf_op jit(solution)/shard_map/ppermute | solution.py:20
  339.0 7.0 %collective-permute-start.35 = (f32[34,34,1]{1,0,2:T(8,128)S(1)}, f32[34,34,1]{1,0,2:T(8,128)S(1)}, u32[]{:S(2)}, u32[]{:S(2)}) collective-permute-start(f32[34,34,1]{1,0,2:T(8,128)S(1)} %copy.365), channel_id=1, source_target_pairs={{0,1},{1,2},{2,3},{3,4},{4,5},{5,6},{6,7},{8,9},{9,10},{10,11},{11... | collective-permute-start | bytes 13880 | tf_op jit(solution)/shard_map/ppermute | solution.py:17
  (26 other events, 195.0 us)
where the time goes:
time: 362 us; the launch traced here: 355 us
  starting transfers between devices  112 us (31%)
  blocking collectives  92.2 us (25%)
  local copies, waits for them, and re-layouts  89.3 us (25%)
  other arithmetic  35.1 us (10%)
  waiting for transfers between devices  24.5 us (7%)
    ppermute x18, starting transfers between devices, extended(): lax.ppermute(lax.slice_in_dim(block, block.shape[dim] - width, None, axis...  81.4 us
    all_to_all x1, blocking collectives, per_device(): lax.all_to_all(diffuse_sent, 'gy', split_axis=0, concat_axis=0, tiled=True)  36.1 us
    all_to_all x1, blocking collectives, per_device(): lax.all_to_all(sol_sent, 'gy', split_axis=0, concat_axis=0, tiled=True)  28.8 us
    all_to_all x1, blocking collectives, per_device(): lax.all_to_all(absorb_sent, 'gy', split_axis=0, concat_axis=0, tiled=True)  27.3 us
    ppermute x18, starting transfers between devices, extended(): lax.ppermute(lax.slice_in_dim(block, 0, width, axis=dim), axis, backward)  27.2 us
    reshape x8, local copies, waits for them, and re-layouts, to_block(): grouped = picked.reshape(BXB, BYB, BZB, box_edge, box_edge, box_edge)  20.6 us
    slice x21, local copies, waits for them, and re-layouts, extended(): lax.slice_in_dim(block, 0, width, axis=dim)  17.8 us
    select_n x4, other arithmetic, per_device(): solution = jnp.where(parity == colour, updated, solution)  14.5 us
  transfers between devices with their start and end apart: 37, of which 13 were waited for; matrix products, arithmetic and copies ran while one was open for 18% of the time, Pallas kernels for 0%

commit v1 on v0

v1 whole, which is shorter than its diff:
```python
import functools
import itertools

import jax
import jax.numpy as jnp
from jax import lax
from jax.experimental import pallas as pl
from jax.experimental.pallas import tpu as pltpu
from jax.sharding import PartitionSpec as P

BOX = 32
N_GX, N_GY, N_GZ = 4, 8, 8
PER_DEV = 4
ROUNDS = 3
HALO = 5
XE = BOX + 2 * HALO
SWEEPS = 2
F32 = jnp.float32
VMEM_LIMIT = 56 * 1024 * 1024


def _colourings():
    table = {}
    for p1, p2 in itertools.combinations(range(1, 7), 2):
        spots = (0, p1, p2)
        for cyc in itertools.product(range(3), repeat=7):
            if any(cyc[p] == cyc[p - 1] for p in range(7)):
                continue
            star = [3 - cyc[p] - cyc[p - 1] for p in spots]
            if len(set(star)) == 3:
                code = sum(c << (2 * i) for i, c in enumerate(list(cyc) + star))
                table[p1 * 7 + p2] = code
                break
    return table


COLOURINGS = _colourings()


def _pick(flag, yes, no):
    return jnp.where(flag, jnp.int32(yes) if isinstance(yes, int) else yes, jnp.int32(no) if isinstance(no, int) else no)


def plan_kernel(corners, f0, f1, f2, f3, plan, pay0, pay1, pay2, own, succ, swap, spot, sems):
    gx, me, gz = lax.axis_index("gx"), lax.axis_index("gy"), lax.axis_index("gz")
    base = gx * (N_GY * N_GZ * PER_DEV) + gz * PER_DEV
    stride = N_GZ * PER_DEV

    def owner(g, s):
        return lax.shift_right_logical(corners[1, base + g * stride + s], 5)

    def inner(g, s):
        return lax.shift_right_logical(corners[2, base + g * stride + s], 5) & 3

    hot = jnp.int32(0)
    rows = []
    for g in range(N_GY):
        row = [owner(g, s) for s in range(PER_DEV)]
        rows.append(row)
        leaving = sum(_pick(o != g, 1, 0) for o in row)
        hot = hot + _pick(leaving == 3, g, 0)
        for s in range(PER_DEV):
            own[g * PER_DEV + s] = row[s]
    first = jnp.int32(0)
    for g in reversed(range(N_GY)):
        to_hot = jnp.int32(0)
        nxt = jnp.int32(0)
        for o in rows[g]:
            to_hot = to_hot + _pick(o == hot, 1, 0)
            nxt = nxt + _pick((o != g) & (o != hot), o, 0)
        is_swap = _pick(hot == g, 0, to_hot)
        succ[g] = nxt
        swap[g] = is_swap
        first = _pick(is_swap == 1, g, first)
    v = first
    p1 = jnp.int32(0)
    p2 = jnp.int32(0)
    mine = jnp.int32(-1)
    pred = jnp.int32(0)
    for p in range(7):
        spot[p] = v
        if p:
            sw = swap[v] == 1
            p2 = _pick(sw & (p1 != 0), p, p2)
            p1 = _pick(sw & (p1 == 0), p, p1)
        mine = _pick(v == me, p, mine)
        pred = _pick(succ[v] == me, v, pred)
        v = succ[v]
    key = p1 * 7 + p2
    code = jnp.int32(0)
    for k, c in COLOURINGS.items():
        code = _pick(key == k, c, code)

    def cycle_colour(p):
        return lax.shift_right_logical(code, 2 * p) & 3

    star = [lax.shift_right_logical(code, 14 + 2 * i) & 3 for i in range(3)]
    spots = [spot[0], spot[p1], spot[p2]]
    is_hot = me == hot
    at = jnp.maximum(mine, 0)
    out_colour = cycle_colour(at)
    in_colour = cycle_colour(_pick(at == 0, 6, at - 1))
    my_succ = succ[me]
    swaps_here = jnp.logical_not(is_hot) & (swap[me] == 1)
    swap_colour = _pick(swaps_here, _pick(at == 0, star[0], _pick(at == p1, star[1], star[2])), -1)
    partners, slots, places, arrives = [], [], [], []
    for k in range(ROUNDS):
        hot_partner = sum(_pick(star[i] == k, spots[i], 0) for i in range(3))
        kind = _pick(swap_colour == k, 3, _pick(out_colour == k, 1, _pick(in_colour == k, 2, 0)))
        partner = _pick(swap_colour == k, hot, _pick(out_colour == k, my_succ, pred))
        kind = _pick(is_hot, 3, kind)
        partner = _pick(is_hot, hot_partner, partner)
        way = me ^ partner
        up = ((kind == 1) & (me < partner)) | ((kind == 2) & (partner < me))
        branch = _pick(kind == 0, 0, _pick(kind == 3, way, _pick(up, 7 + way, 14 + way)))
        plan[k] = branch
        slot = jnp.int32(0)
        place = jnp.int32(0)
        for s in range(PER_DEV):
            slot = slot + _pick(own[me * PER_DEV + s] == partner, s, 0)
            place = place + _pick(own[partner * PER_DEV + s] == me, inner(partner, s), 0)
        slot = jnp.minimum(slot, PER_DEV - 1)
        slots.append(slot)
        places.append(place)
        arrives.append((kind == 2) | (kind == 3))
    fields = (f0, f1, f2, f3)
    pays = (pay0, pay1, pay2)
    copies = [
        pltpu.make_async_copy(fields[f].at[slots[k]], pays[k].at[f], sems.at[k, f])
        for k in range(ROUNDS)
        for f in range(4)
    ]
    for copy in copies:
        copy.start()
    for q in range(PER_DEV):
        source = jnp.int32(0)
        for s in range(PER_DEV):
            source = source + _pick((own[me * PER_DEV + s] == me) & (inner(me, s) == q), s, 0)
        for k in range(ROUNDS):
            source = source + _pick(arrives[k] & (places[k] == q), 4 + k, 0)
        plan[4 + q] = source
    plan[3] = jnp.int32(0)
    for copy in copies:
        copy.wait()


def plan_and_pack(corners, fields):
    any_spec = pl.BlockSpec(memory_space=pl.ANY)
    smem = pl.BlockSpec(memory_space=pltpu.SMEM)
    pay = jax.ShapeDtypeStruct((4,) + fields[0].shape[1:], F32)
    return pl.pallas_call(
        plan_kernel,
        out_shape=(jax.ShapeDtypeStruct((8,), jnp.int32), pay, pay, pay),
        in_specs=[smem] + [any_spec] * 4,
        out_specs=(smem, any_spec, any_spec, any_spec),
        scratch_shapes=[
            pltpu.SMEM((32,), jnp.int32),
            pltpu.SMEM((8,), jnp.int32),
            pltpu.SMEM((8,), jnp.int32),
            pltpu.SMEM((8,), jnp.int32),
            pltpu.SemaphoreType.DMA((ROUNDS, 4)),
        ],
        name="plan",
    )(corners, *fields)


def swap_round(branch, pay):
    def stay(x):
        return x

    def move(pairs, x):
        return lax.ppermute(x, "gy", pairs)

    branches = [stay]
    for r in range(1, 8):
        branches.append(functools.partial(move, [(i, i ^ r) for i in range(8)]))
    for r in range(1, 8):
        branches.append(functools.partial(move, [(i, i ^ r) for i in range(8) if i < i ^ r]))
    for r in range(1, 8):
        branches.append(functools.partial(move, [(i, i ^ r) for i in range(8) if i > i ^ r]))
    return lax.switch(branch, branches, pay)


def iota(dim):
    return lax.broadcasted_iota(jnp.int32, (8, 128), dim)


def lroll(v, shift):
    shift %= 128
    return pltpu.roll(v, shift, 1) if shift else v


def sroll(v, shift):
    shift %= 8
    return pltpu.roll(v, shift, 0) if shift else v


def assemble_kernel(plan, f0, f1, f2, f3, r0, r1, r2, home, even, odd, raw, tmp, sems):
    fields = (f0, f1, f2, f3)
    gots = (r0, r1, r2)
    for q in range(PER_DEV):
        source = plan[4 + q]

        @pl.when(source < 4)
        def _():
            for f in range(4):
                pltpu.make_async_copy(fields[f].at[jnp.minimum(source, 3)], raw.at[f, q], sems.at[f, q]).start()

        for k in range(ROUNDS):

            @pl.when(source == 4 + k)
            def _():
                for f in range(4):
                    pltpu.make_async_copy(gots[k].at[f], raw.at[f, q], sems.at[f, q]).start()

    for q in range(PER_DEV):
        for f in range(4):
            pltpu.make_async_copy(f0.at[0], raw.at[f, q], sems.at[f, q]).wait()

    lane = iota(1)
    m64 = (lane & 64) != 0
    m32 = (lane & 32) != 0

    def step(i, carry):
        f = i // 4
        xt = pl.multiple_of((i % 4) * 8, 8)
        for t in range(4):
            for jj in range(2):
                j = 2 * t + jj
                a = [raw[f, k, pl.ds(xt, 8), j * 128 : (j + 1) * 128] for k in range(4)]
                n0 = jnp.where(m64, lroll(a[2], 64), a[0])
                n2 = jnp.where(m64, a[2], lroll(a[0], 64))
                n1 = jnp.where(m64, lroll(a[3], 64), a[1])
                n3 = jnp.where(m64, a[3], lroll(a[1], 64))
                b = [
                    jnp.where(m32, lroll(n1, 32), n0),
                    jnp.where(m32, n1, lroll(n0, 96)),
                    jnp.where(m32, lroll(n3, 32), n2),
                    jnp.where(m32, n3, lroll(n2, 96)),
                ]
                for q in range(4):
                    y = jj * 4 + q
                    tmp[t, y * 8 : y * 8 + 8, :] = b[q]
            for x in range(8):
                home[f, xt + x, t * 8 : t * 8 + 8, :] = tmp[t, pl.ds(x, 8, stride=8), :]
        return carry

    lax.fori_loop(0, 16, step, 0)

    low = (lax.axis_index("gx") & 1) == 1
    base = iota(0) + lane
    for t in range(4):
        ys = slice(t * 8, t * 8 + 8)

        def put(n, lo, hi):
            even[n, ys, :] = jnp.where(low, lo, hi)
            odd[n, ys, :] = jnp.where(low, hi, lo)

        for n in range(3):
            pair = []
            for x in (n, 27 + n):
                here = home[0, x, ys, :]
                if n < 2:
                    here = jnp.where(((base + x) & 1) == 1, here, home[0, x + 3, ys, :])
                pair.append(here)
            put(n, *pair)
        for n in range(5):
            put(3 + n, home[3, n, ys, :], home[3, 27 + n, ys, :])
        for n in range(4):
            put(8 + n, home[1, n, ys, :], home[1, 28 + n, ys, :])
            put(12 + n, home[2, n, ys, :], home[2, 28 + n, ys, :])


def assemble(plan, fields, gots):
    any_spec = pl.BlockSpec(memory_space=pl.ANY)
    vmem = pl.BlockSpec(memory_space=pltpu.VMEM)
    face = jax.ShapeDtypeStruct((16, BOX, 128), F32)
    return pl.pallas_call(
        assemble_kernel,
        out_shape=(jax.ShapeDtypeStruct((4, BOX, BOX, 128), F32), face, face),
        in_specs=[pl.BlockSpec(memory_space=pltpu.SMEM)] + [any_spec] * 7,
        out_specs=(vmem, vmem, vmem),
        scratch_shapes=[
            pltpu.VMEM((4, PER_DEV, BOX, BOX * BOX), F32),
            pltpu.VMEM((4, 64, 128), F32),
            pltpu.SemaphoreType.DMA((4, PER_DEV)),
        ],
        compiler_params=pltpu.CompilerParams(vmem_limit_bytes=VMEM_LIMIT),
        name="assemble",
    )(plan, *fields, *gots)


def sides(axis, count):
    i = lax.axis_index(axis)
    return (i & 1) == 1, i > 0, i < count - 1


def halo_of(axis, count, even, odd):
    low_first, has_low, has_high = sides(axis, count)
    low = jnp.where(has_low, jnp.where(low_first, even, odd), 0.0)
    high = jnp.where(has_high, jnp.where(low_first, odd, even), 0.0)
    return low, high


def x_halo_tiles(even, odd, t):
    ys = slice(t * 8, t * 8 + 8)
    layers = [halo_of("gx", N_GX, even[n, ys, :], odd[n, ys, :]) for n in range(16)]
    planes = {}
    for side in range(2):
        part = [layer[side] for layer in layers]
        for i in range(HALO):
            j = i - 1 if side == 0 else i
            inside = 0 <= j < 4
            u = part[i % 3]
            planes[i if side == 0 else HALO + BOX + i] = (
                u,
                part[8 + j] if inside else None,
                part[12 + j] if inside else None,
                part[3 + i],
            )
    return planes


def pack_y(u, f, a, b, colour1, high):
    sub = iota(0)
    pair = jnp.where(colour1, u, sroll(u, -3))
    if high:
        first = jnp.where(sub < 3, sroll(pair, -3), b)
        second = jnp.where(sub < 4, sroll(f, -4), a)
    else:
        first = jnp.where(sub < 3, pair, sroll(b, 3))
        second = jnp.where(sub < 4, f, sroll(a, 4))
    return first, second


def pack_y_kernel(home, x_even, x_odd, even, odd):
    low = (lax.axis_index("gy") & 1) == 1
    base = iota(0) + iota(1)

    def put(e, tiles, colour1):
        lo = pack_y(*tiles[0], colour1, False)
        hi = pack_y(*tiles[1], colour1, True)
        for n in range(2):
            even[e, n * 8 : n * 8 + 8, :] = jnp.where(low, lo[n], hi[n])
            odd[e, n * 8 : n * 8 + 8, :] = jnp.where(low, hi[n], lo[n])

    def step(x, carry):
        colour1 = ((base + x) & 1) == 1
        put(x + HALO, [[home[f, x, t * 8 : t * 8 + 8, :] for f in range(4)] for t in (0, 3)], colour1)
        return carry

    lax.fori_loop(0, BOX, step, 0)
    near, far = x_halo_tiles(x_even, x_odd, 0), x_halo_tiles(x_even, x_odd, 3)
    zero = jnp.zeros((8, 128), F32)
    for e in near:
        colour1 = ((base + e + 1) & 1) == 1
        put(e, [[zero if v is None else v for v in tiles[e]] for tiles in (near, far)], colour1)


def build_main(home, x_even, x_odd, y_even, y_odd, ub, fa):
    def step(x, carry):
        ub[0, x + HALO, 16:48, :] = home[0, x]
        ub[1, x + HALO, 16:48, :] = home[3, x]
        fa[0, x + HALO, 8:40, :] = home[1, x]
        fa[1, x + HALO, 8:40, :] = home[2, x]
        return carry

    lax.fori_loop(0, BOX, step, 0)
    zero = jnp.zeros((8, 128), F32)
    for t in range(4):
        for e, (u, f, a, b) in x_halo_tiles(x_even, x_odd, t).items():
            ub[0, e, 16 + t * 8 : 24 + t * 8, :] = u
            ub[1, e, 16 + t * 8 : 24 + t * 8, :] = b
            fa[0, e, 8 + t * 8 : 16 + t * 8, :] = zero if f is None else f
            fa[1, e, 8 + t * 8 : 16 + t * 8, :] = zero if a is None else a
    sub = iota(0)

    def halo(e, carry):
        l0, h0 = halo_of("gy", N_GY, y_even[e, 0:8, :], y_odd[e, 0:8, :])
        l1, h1 = halo_of("gy", N_GY, y_even[e, 8:16, :], y_odd[e, 8:16, :])
        ub[0, e, 0:8, :] = zero
        ub[1, e, 0:8, :] = zero
        ub[0, e, 8:16, :] = jnp.where(sub < 6, sroll(l0, 3), sroll(l0, 6))
        ub[1, e, 8:16, :] = l0
        fa[0, e, 0:8, :] = sroll(l1, 4)
        fa[1, e, 0:8, :] = l1
        ub[0, e, 48:56, :] = jnp.where(sub < 3, h0, sroll(h0, 3))
        ub[1, e, 48:56, :] = sroll(h0, -3)
        fa[0, e, 40:48, :] = h1
        fa[1, e, 40:48, :] = sroll(h1, 4)
        ub[0, e, 56:64, :] = zero
        ub[1, e, 56:64, :] = zero
        return carry

    lax.fori_loop(0, XE, halo, 0)


def pack_z_kernel(home, x_even, x_odd, y_even, y_odd, ub, fa, even, odd):
    build_main(home, x_even, x_odd, y_even, y_odd, ub, fa)
    low = (lax.axis_index("gz") & 1) == 1
    lane = iota(1)
    base = iota(0) + lane
    place = lane & 15
    group = lax.shift_right_logical(lane, 4)

    def step(e, carry):
        colour1 = ((base + e + 1) & 1) == 1
        lo = jnp.zeros((8, 128), F32)
        hi = lo
        for t in range(6):
            u = ub[0, e, 8 + t * 8 : 16 + t * 8, :]
            b = ub[1, e, 8 + t * 8 : 16 + t * 8, :]
            f = fa[0, e, t * 8 : 8 + t * 8, :]
            a = fa[1, e, t * 8 : 8 + t * 8, :]
            pair = jnp.where(colour1, u, lroll(u, -3))
            o = 16 * t

            def join(p, bb, ff, aa):
                return jnp.where(place < 3, p, jnp.where(place < 8, bb, jnp.where(place < 12, ff, aa)))

            g = join(lroll(pair, o), lroll(b, o + 3), lroll(f, o + 8), lroll(a, o + 12))
            lo = jnp.where(group == t, g, lo)
            g = join(lroll(pair, o + 5), lroll(b, o + 8), lroll(f, o + 12), lroll(a, o + 16))
            hi = jnp.where(group == t, g, hi)
        even[e] = jnp.where(low, lo, hi)
        odd[e] = jnp.where(low, hi, lo)
        return carry

    lax.fori_loop(0, XE, step, 0)


def shifted_z(main, aux, lane, first, last):
    m, a = lroll(main, 1), lroll(aux, 1)
    below = (jnp.where(first, a, m), jnp.where(first, m, a))
    m, a = lroll(main, 127), lroll(aux, 127)
    above = (jnp.where(last, a, m), jnp.where(last, m, a))
    return below, above


def sweep_kernel(ub, fa, z_even, z_odd, sol, res, u, b, fx, co, dg):
    lane = iota(1)
    first, last = lane == 0, lane == 127
    base = iota(0) + lane
    zero = jnp.zeros((8, 128), F32)

    def unpack(e, carry):
        lo, hi = halo_of("gz", N_GZ, z_even[e], z_odd[e])
        for w in (0, 56):
            u[1, e, w : w + 8, :] = zero
            b[1, e, w : w + 8, :] = zero
        u[0, e] = ub[0, e]
        b[0, e] = ub[1, e]
        for t in range(6):
            o = 16 * t
            rows = slice(8 + t * 8, 16 + t * 8)
            part = jnp.where(lane < 3, lroll(hi, -o), lroll(hi, 3 - o))
            part = jnp.where(lane < 64, part, jnp.where(lane < 126, lroll(lo, 123 - o), lroll(lo, 126 - o)))
            u[1, e, rows, :] = part
            b[1, e, rows, :] = jnp.where(lane < 64, lroll(hi, -3 - o), lroll(lo, 120 - o))
            rows = slice(t * 8, 8 + t * 8)
            fx[0, e, rows, :] = jnp.where(lane < 64, lroll(hi, -8 - o), lroll(lo, 116 - o))
            fx[1, e, rows, :] = jnp.where(lane < 64, lroll(hi, -12 - o), lroll(lo, 112 - o))
        return carry

    lax.fori_loop(0, XE, unpack, 0)

    def coefs(e, carry):
        for t in range(6):
            r = 8 + t * 8
            rows = slice(t * 8, 8 + t * 8)
            mid = [b[s, e, r : r + 8, :] for s in range(2)]
            below, above = shifted_z(mid[0], mid[1], lane, first, last)
            for s in range(2):
                near = (
                    b[s, e - 1, r : r + 8, :],
                    b[s, e + 1, r : r + 8, :],
                    b[s, e, r - 1 : r + 7, :],
                    b[s, e, r + 1 : r + 9, :],
                    below[s],
                    above[s],
                )
                faces = [0.5 * (mid[s] + v) for v in near]
                f, a = (fa, fx)[s][0, e, rows, :], (fa, fx)[s][1, e, rows, :]
                diag = a + (faces[1] + faces[0]) + (faces[3] + faces[2]) + (faces[5] + faces[4])
                inverse = jnp.where(mid[s] > 0, 1.0 / diag, 0.0)
                for n in range(6):
                    co[s, n, e - 1, rows, :] = faces[n] * inverse
                co[s, 6, e - 1, rows, :] = f * inverse
                if s == 0 and 1 <= t <= 4:
                    dg[e - 1, (t - 1) * 8 : t * 8, :] = diag
        return carry

    lax.fori_loop(1, XE - 1, coefs, 0)

    def update(e, t, spans):
        r = 8 + t * 8
        rows = slice(t * 8, 8 + t * 8)
        mid = [u[s, e, r : r + 8, :] for s in range(2)]
        below, above = shifted_z(mid[0], mid[1], lane, first, last)
        new = []
        for s in spans:
            c = [co[s, n, e - 1, rows, :] for n in range(7)]
            x = c[0] * u[s, e - 1, r : r + 8, :] + c[1] * u[s, e + 1, r : r + 8, :]
            y = c[2] * u[s, e, r - 1 : r + 7, :] + c[3] * u[s, e, r + 1 : r + 9, :]
            z = c[4] * below[s] + c[5] * above[s]
            new.append(c[6] + ((x + y) + z))
        return mid, new

    for half in range(2 * SWEEPS):
        colour = half % 2

        def sweep(e, carry):
            hit = ((base + e + 1) & 1) == colour
            for t in range(6):
                r = 8 + t * 8
                mid, new = update(e, t, (0, 1))
                for s in range(2):
                    u[s, e, r : r + 8, :] = jnp.where(hit, new[s], mid[s])
            return carry

        lax.fori_loop(1 + half, XE - 1 - half, sweep, 0)

    def finish(e, carry):
        for t in range(1, 5):
            mid, new = update(e, t, (0,))
            rows = slice((t - 1) * 8, t * 8)
            sol[e - HALO, rows, :] = mid[0]
            res[e - HALO, rows, :] = dg[e - 1, rows, :] * (new[0] - mid[0])
        return carry

    lax.fori_loop(HALO, HALO + BOX, finish, 0)


def on_vmem(kernel, out_shape, scratch, name, *args):
    vmem = pl.BlockSpec(memory_space=pltpu.VMEM)
    return pl.pallas_call(
        kernel,
        out_shape=out_shape,
        in_specs=[vmem] * len(args),
        out_specs=tuple([vmem] * len(out_shape)),
        scratch_shapes=scratch,
        compiler_params=pltpu.CompilerParams(vmem_limit_bytes=VMEM_LIMIT),
        name=name,
    )(*args)


def exchange(axis, count, even, odd):
    pairs = []
    for start in (0, 1):
        step = []
        for i in range(start, count, 2):
            j = (i + 1) % count
            step += [(i, j), (j, i)]
        pairs.append(step)
    return lax.ppermute(even, axis, pairs[0]), lax.ppermute(odd, axis, pairs[1])


def per_device(solution_old, right_side, acoef, bcoef, corners):
    fields = (solution_old, right_side, acoef, bcoef)
    plan, *pays = plan_and_pack(corners, fields)
    gots = [swap_round(plan[k], pays[k]) for k in range(ROUNDS)]
    home, even, odd = assemble(plan, fields, gots)
    x_even, x_odd = exchange("gx", N_GX, even, odd)
    face = jax.ShapeDtypeStruct((XE, 16, 128), F32)
    even, odd = on_vmem(pack_y_kernel, (face, face), [], "pack_y", home, x_even, x_odd)
    y_even, y_odd = exchange("gy", N_GY, even, odd)
    face = jax.ShapeDtypeStruct((XE, 8, 128), F32)
    ub, fa, even, odd = on_vmem(
        pack_z_kernel,
        (jax.ShapeDtypeStruct((2, XE, 64, 128), F32), jax.ShapeDtypeStruct((2, XE, 48, 128), F32), face, face),
        [],
        "pack_z",
        home,
        x_even,
        x_odd,
        y_even,
        y_odd,
    )
    z_even, z_odd = exchange("gz", N_GZ, even, odd)
    block = jax.ShapeDtypeStruct((BOX, BOX, 128), F32)
    return on_vmem(
        sweep_kernel,
        (block, block),
        [
            pltpu.VMEM((2, XE, 64, 128), F32),
            pltpu.VMEM((2, XE, 64, 128), F32),
            pltpu.VMEM((2, XE, 48, 128), F32),
            pltpu.VMEM((2, 7, XE - 2, 48, 128), F32),
            pltpu.VMEM((XE - 2, BOX, 128), F32),
        ],
        "sweeps",
        ub,
        fa,
        z_even,
        z_odd,
    )


def solution(mesh):
    boxes = P(("gx", "gy", "gz"), None, None)
    block = P("gx", "gy", "gz")
    return jax.shard_map(
        per_device,
        mesh=mesh,
        in_specs=(boxes, boxes, boxes, boxes, P()),
        out_specs=(block, block),
        check_vma=False,
    )
```

time: 362 us -> 161 us (0.44)
  the two profiles are of different devices: /device:TPU:1 before, /device:TPU:87 now
where the time goes in v1:
time: 161 us; the launch traced here: 158 us
  Pallas kernels  63.1 us (39%)
  starting transfers between devices  57.4 us (36%)
  waiting for transfers between devices  31.4 us (20%)
  local copies, waits for them, and re-layouts  3.53 us (2%)
  between operations  2.62 us (2%)
    pallas_call x3, Pallas kernels, on_vmem(): pl.pallas_call(kernel, out_shape=out_shape, in_specs=[vmem] * len(args),...  52.4 us
    ppermute x3, starting transfers between devices, exchange(): lax.ppermute(odd, axis, pairs[1])  28.5 us
    ppermute x2, starting transfers between devices, move(): return lax.ppermute(x, 'gy', pairs)  22.8 us
    ppermute x2, waiting for transfers between devices, move(): return lax.ppermute(x, 'gy', pairs)  16.9 us
    ppermute x3, waiting for transfers between devices, exchange(): lax.ppermute(odd, axis, pairs[1])  13.7 us
    pallas_call x1, Pallas kernels, assemble(): pl.pallas_call(assemble_kernel, out_shape=(jax.ShapeDtypeStruct((4, BOX,...  7.33 us
    ppermute x3, starting transfers between devices, exchange(): lax.ppermute(even, axis, pairs[0])  6.09 us
    pallas_call x1, Pallas kernels, plan_and_pack(): pl.pallas_call(plan_kernel, out_shape=(jax.ShapeDtypeStruct((8,), jnp.int...  3.33 us
  transfers between devices with their start and end apart: 8, of which 6 were waited for; matrix products, arithmetic and copies ran while one was open for 0% of the time, Pallas kernels for 0%

profile of v1, /device:TPU:87, one launch (start us, length us, event | category | flops | bytes accessed | tf_op | source)
XLA Modules:
  0.0 158.4 jit_solution(17163913920344900961)
XLA Ops:
  0.6 3.3 %plan.1 = (s32[8]{0:T(128)}, f32[4,32,1024]{2,1,0:T(8,128)S(1)}, f32[4,32,1024]{2,1,0:T(8,128)S(1)}, f32[4,32,1024]{2,1,0:T(8,128)S(1)}) custom-call(s32[3,1024]{1,0:T(4,128)} %corners.1, f32[4,32,1024]{2,1,0:T(8,128)} %f0.3, f32[4,32,1024]{2,1,0:T(8,128)} %f1.3, f32[4,32,1024]{2,1,0:T(8,128)} %f2.3, f32[4,32,1024]{2,1,0:T(8,128)} %f3.3), custom_call_target="tpu_custom_call" | custom-call | tf_op jit(solution)/shard_map/plan/pallas_call | solution.py:151
  4.0 1.3 fusion
  7.3 29.1 %conditional.4 = (f32[4,32,1024]{2,1,0:T(8,128)S(1)}) conditional(s32[]{:T(128)} %bitcast.1, f32[4,32,1024]{2,1,0:T(8,128)S(1)} %get-tuple-element.152, f32[4,32,1024]{2,1,0:T(8,128)S(1)} %get-tuple-element.152, f32[4,32,1024]{2,1,0:T(8,128)S(1)} %get-tuple-element.152, ...), branch_computations={%region_22.0_spmd, %region_23.0_spmd, %region_24.0_spmd, %region_2... | conditional | bytes 3145776 | solution.py:181
  7.3 21.5 %collective-permute-start.31 = (f32[4,32,1024]{2,1,0:T(8,128)S(1)}, f32[4,32,1024]{2,1,0:T(8,128)S(1)}, u32[]{:S(2)}, u32[]{:S(2)}) collective-permute-start(f32[4,32,1024]{2,1,0:T(8,128)S(1)} %param.33), channel_id=1, source_target_pairs={{0,32},{8,40},{16,48},{24,56},{1,33},{9,41},{17,49},{25,57},{2,34}... | collective-permute-start | bytes 1572872 | tf_op jit(solution)/shard_map/cond/branch_11_fun/ppermute | solution.py:172
  28.8 7.3 %collective-permute-done.31 = f32[4,32,1024]{2,1,0:T(8,128)S(1)} collective-permute-done((f32[4,32,1024]{2,1,0:T(8,128)S(1)}, f32[4,32,1024]{2,1,0:T(8,128)S(1)}, u32[]{:S(2)}, u32[]{:S(2)}) %collective-permute-start.31) | collective-permute-done | bytes 524320 | tf_op jit(solution)/shard_map/cond/branch_11_fun/ppermute | solution.py:172
  36.4 11.0 %conditional.3 = (f32[4,32,1024]{2,1,0:T(8,128)S(1)}) conditional(s32[]{:T(128)} %bitcast, f32[4,32,1024]{2,1,0:T(8,128)S(1)} %get-tuple-element.151, f32[4,32,1024]{2,1,0:T(8,128)S(1)} %get-tuple-element.151, f32[4,32,1024]{2,1,0:T(8,128)S(1)} %get-tuple-element.151, ...), branch_computations={%region_0.0_spmd, %region_1.0_spmd, %region_2.0_spmd, %region_3.0_... | conditional | bytes 3145776 | solution.py:181
  36.4 1.3 collective-permute-start.8
  37.7 9.6 %collective-permute-done.8 = f32[4,32,1024]{2,1,0:T(8,128)S(1)} collective-permute-done((f32[4,32,1024]{2,1,0:T(8,128)S(1)}, f32[4,32,1024]{2,1,0:T(8,128)S(1)}, u32[]{:S(2)}, u32[]{:S(2)}) %collective-permute-start.8) | collective-permute-done | bytes 524320 | tf_op jit(solution)/shard_map/cond/branch_9_fun/ppermute | solution.py:172
  47.4 7.3 %assemble.1 = (f32[4,32,32,128]{3,2,1,0:T(8,128)}, f32[16,32,128]{2,1,0:T(8,128)}, f32[16,32,128]{2,1,0:T(8,128)}) custom-call(s32[8]{0:T(128)} %get-tuple-element.150.plan, f32[4,32,1024]{2,1,0:T(8,128)} %f0.3, f32[4,32,1024]{2,1,0:T(8,128)} %f1.3, f32[4,32,1024]{2,1,0:T(8,128)} %f2.3, f32[4,32,1024]{2,1,0:T(8,128)} %f3.3, ...), custom_call_target="tpu_custom_call" | custom-call | tf_op jit(solution)/shard_map/assemble/pallas_call | solution.py:278
  54.7 0.5 collective-permute-start.63
  55.3 10.6 %collective-permute-start.64 = (f32[16,32,128]{2,1,0:T(8,128)}, f32[16,32,128]{2,1,0:T(8,128)S(1)}, u32[]{:S(2)}, u32[]{:S(2)}) collective-permute-start(f32[16,32,128]{2,1,0:T(8,128)} %get-tuple-element.156), channel_id=1, source_target_pairs={{64,128},{128,64},{192,0},{0,192},{65,129},{129,65},{193,1},{1,193... | collective-permute-start | bytes 786440 | tf_op jit(solution)/shard_map/ppermute | solution.py:555
  65.9 5.5 %collective-permute-done.64.x_odd = f32[16,32,128]{2,1,0:T(8,128)S(1)} collective-permute-done((f32[16,32,128]{2,1,0:T(8,128)}, f32[16,32,128]{2,1,0:T(8,128)S(1)}, u32[]{:S(2)}, u32[]{:S(2)}) %collective-permute-start.64) | collective-permute-done | bytes 262176 | tf_op jit(solution)/shard_map/ppermute | solution.py:555
  71.5 0.7 copy-done.1
  72.2 2.8 %pack_y.1 = (f32[42,16,128]{2,1,0:T(8,128)}, f32[42,16,128]{2,1,0:T(8,128)}) custom-call(f32[4,32,32,128]{3,2,1,0:T(8,128)} %get-tuple-element.154.home, f32[16,32,128]{2,1,0:T(8,128)} %copy-done, f32[16,32,128]{2,1,0:T(8,128)} %copy-done.1), custom_call_target="tpu_custom_call" | custom-call | tf_op jit(solution)/shard_map/pack_y/pallas_call | solution.py:536
  75.0 5.5 %collective-permute-start.65 = (f32[42,16,128]{2,1,0:T(8,128)}, f32[42,16,128]{2,1,0:T(8,128)S(1)}, u32[]{:S(2)}, u32[]{:S(2)}) collective-permute-start(f32[42,16,128]{2,1,0:T(8,128)} %get-tuple-element.157), channel_id=1, source_target_pairs={{0,8},{8,0},{16,24},{24,16},{32,40},{40,32},{48,56},{56,48},{1,9},... | collective-permute-start | bytes 1032200 | tf_op jit(solution)/shard_map/ppermute | solution.py:555
  80.5 6.4 %collective-permute-start.66 = (f32[42,16,128]{2,1,0:T(8,128)}, f32[42,16,128]{2,1,0:T(8,128)S(1)}, u32[]{:S(2)}, u32[]{:S(2)}) collective-permute-start(f32[42,16,128]{2,1,0:T(8,128)} %get-tuple-element.158), channel_id=1, source_target_pairs={{8,16},{16,8},{24,32},{32,24},{40,48},{48,40},{56,0},{0,56},{9,17}... | collective-permute-start | bytes 1032200 | tf_op jit(solution)/shard_map/ppermute | solution.py:555
  86.9 0.7 collective-permute-done.65.y_even
  87.7 4.9 %collective-permute-done.66.y_odd = f32[42,16,128]{2,1,0:T(8,128)S(1)} collective-permute-done((f32[42,16,128]{2,1,0:T(8,128)}, f32[42,16,128]{2,1,0:T(8,128)S(1)}, u32[]{:S(2)}, u32[]{:S(2)}) %collective-permute-start.66) | collective-permute-done | bytes 344096 | tf_op jit(solution)/shard_map/ppermute | solution.py:555
  92.6 0.7 copy-done.3
  93.3 11.2 %pack_z.1 = (f32[2,42,64,128]{3,2,1,0:T(8,128)}, f32[2,42,48,128]{3,2,1,0:T(8,128)}, f32[42,8,128]{2,1,0:T(8,128)}, f32[42,8,128]{2,1,0:T(8,128)}) custom-call(f32[4,32,32,128]{3,2,1,0:T(8,128)} %get-tuple-element.154.home, f32[16,32,128]{2,1,0:T(8,128)} %copy-done, f32[16,32,128]{2,1,0:T(8,128)} %copy-done.1, f32[42,16,128]{2,1,0:T(8,128)} %copy-done.2, ...), custom_call_target="tpu_custom_call" | custom-call | tf_op jit(solution)/shard_map/pack_z/pallas_call | solution.py:536
  104.5 11.5 %collective-permute-start.68 = (f32[42,8,128]{2,1,0:T(8,128)}, f32[42,8,128]{2,1,0:T(8,128)S(1)}, u32[]{:S(2)}, u32[]{:S(2)}) collective-permute-start(f32[42,8,128]{2,1,0:T(8,128)} %get-tuple-element.162), channel_id=1, source_target_pairs={{1,2},{2,1},{3,4},{4,3},{5,6},{6,5},{7,0},{0,7},{9,10},{10,9},{11,... | collective-permute-start | bytes 516104 | tf_op jit(solution)/shard_map/ppermute | solution.py:555
  116.0 3.3 %collective-permute-done.68.z_odd = f32[42,8,128]{2,1,0:T(8,128)S(1)} collective-permute-done((f32[42,8,128]{2,1,0:T(8,128)}, f32[42,8,128]{2,1,0:T(8,128)S(1)}, u32[]{:S(2)}, u32[]{:S(2)}) %collective-permute-start.68) | collective-permute-done | bytes 172064 | tf_op jit(solution)/shard_map/ppermute | solution.py:555
  119.3 0.7 copy-done.5
  120.0 38.4 %sweeps.1 = (f32[32,32,128]{2,1,0:T(8,128)}, f32[32,32,128]{2,1,0:T(8,128)}) custom-call(f32[2,42,64,128]{3,2,1,0:T(8,128)} %get-tuple-element.159.ub, f32[2,42,48,128]{3,2,1,0:T(8,128)} %get-tuple-element.160.fa, f32[42,8,128]{2,1,0:T(8,128)} %copy-done.4, f32[42,8,128]{2,1,0:T(8,128)} %copy-done.5), custom_call_target="tpu_custom_call" | custom-call | tf_op jit(solution)/shard_map/sweeps/pallas_call | solution.py:536
  (15 shorter events, 0.1 us)
Async XLA Ops:
  7.3 28.8 %collective-permute-start.31 = (f32[4,32,1024]{2,1,0:T(8,128)S(1)}, f32[4,32,1024]{2,1,0:T(8,128)S(1)}, u32[]{:S(2)}, u32[]{:S(2)}) collective-permute-start(f32[4,32,1024]{2,1,0:T(8,128)S(1)} %param.33), channel_id=1, source_target_pairs={{0,32},{8,40},{16,48},{24,56},{1,33},{9,41},{17,49},{25,57},{2,34}... | collective-permute-start | bytes 1572872 | tf_op jit(solution)/shard_map/cond/branch_11_fun/ppermute | solution.py:172
  36.4 10.9 %collective-permute-start.8 = (f32[4,32,1024]{2,1,0:T(8,128)S(1)}, f32[4,32,1024]{2,1,0:T(8,128)S(1)}, u32[]{:S(2)}, u32[]{:S(2)}) collective-permute-start(f32[4,32,1024]{2,1,0:T(8,128)S(1)} %param.9), channel_id=1, source_target_pairs={{0,16},{8,24},{32,48},{40,56},{1,17},{9,25},{33,49},{41,57},{2,18}... | collective-permute-start | bytes 1572872 | tf_op jit(solution)/shard_map/cond/branch_9_fun/ppermute | solution.py:172
  54.7 11.2 %collective-permute-start.63 = (f32[16,32,128]{2,1,0:T(8,128)}, f32[16,32,128]{2,1,0:T(8,128)S(1)}, u32[]{:S(2)}, u32[]{:S(2)}) collective-permute-start(f32[16,32,128]{2,1,0:T(8,128)} %get-tuple-element.155), channel_id=1, source_target_pairs={{0,64},{64,0},{128,192},{192,128},{1,65},{65,1},{129,193},{193,129... | collective-permute-start | bytes 786440 | tf_op jit(solution)/shard_map/ppermute | solution.py:555
  55.3 16.2 %collective-permute-start.64 = (f32[16,32,128]{2,1,0:T(8,128)}, f32[16,32,128]{2,1,0:T(8,128)S(1)}, u32[]{:S(2)}, u32[]{:S(2)}) collective-permute-start(f32[16,32,128]{2,1,0:T(8,128)} %get-tuple-element.156), channel_id=1, source_target_pairs={{64,128},{128,64},{192,0},{0,192},{65,129},{129,65},{193,1},{1,193... | collective-permute-start | bytes 786440 | tf_op jit(solution)/shard_map/ppermute | solution.py:555
  65.9 5.5 %copy-start = (f32[16,32,128]{2,1,0:T(8,128)}, f32[16,32,128]{2,1,0:T(8,128)S(1)}, u32[]{:S(2)}) copy-start(f32[16,32,128]{2,1,0:T(8,128)S(1)} %collective-permute-done.63.x_even) | copy-start | bytes 786436
  71.5 0.7 copy-start.1
  75.0 12.7 %collective-permute-start.65 = (f32[42,16,128]{2,1,0:T(8,128)}, f32[42,16,128]{2,1,0:T(8,128)S(1)}, u32[]{:S(2)}, u32[]{:S(2)}) collective-permute-start(f32[42,16,128]{2,1,0:T(8,128)} %get-tuple-element.157), channel_id=1, source_target_pairs={{0,8},{8,0},{16,24},{24,16},{32,40},{40,32},{48,56},{56,48},{1,9},... | collective-permute-start | bytes 1032200 | tf_op jit(solution)/shard_map/ppermute | solution.py:555
  80.5 12.1 %collective-permute-start.66 = (f32[42,16,128]{2,1,0:T(8,128)}, f32[42,16,128]{2,1,0:T(8,128)S(1)}, u32[]{:S(2)}, u32[]{:S(2)}) collective-permute-start(f32[42,16,128]{2,1,0:T(8,128)} %get-tuple-element.158), channel_id=1, source_target_pairs={{8,16},{16,8},{24,32},{32,24},{40,48},{48,40},{56,0},{0,56},{9,17}... | collective-permute-start | bytes 1032200 | tf_op jit(solution)/shard_map/ppermute | solution.py:555
  87.7 4.9 %copy-start.2 = (f32[42,16,128]{2,1,0:T(8,128)}, f32[42,16,128]{2,1,0:T(8,128)S(1)}, u32[]{:S(2)}) copy-start(f32[42,16,128]{2,1,0:T(8,128)S(1)} %collective-permute-done.65.y_even) | copy-start | bytes 1032196
  92.6 0.7 copy-start.3
  104.5 11.5 %collective-permute-start.67 = (f32[42,8,128]{2,1,0:T(8,128)}, f32[42,8,128]{2,1,0:T(8,128)S(1)}, u32[]{:S(2)}, u32[]{:S(2)}) collective-permute-start(f32[42,8,128]{2,1,0:T(8,128)} %get-tuple-element.161), channel_id=1, source_target_pairs={{0,1},{1,0},{2,3},{3,2},{4,5},{5,4},{6,7},{7,6},{8,9},{9,8},{10,11... | collective-permute-start | bytes 516104 | tf_op jit(solution)/shard_map/ppermute | solution.py:555
  104.5 14.8 %collective-permute-start.68 = (f32[42,8,128]{2,1,0:T(8,128)}, f32[42,8,128]{2,1,0:T(8,128)S(1)}, u32[]{:S(2)}, u32[]{:S(2)}) collective-permute-start(f32[42,8,128]{2,1,0:T(8,128)} %get-tuple-element.162), channel_id=1, source_target_pairs={{1,2},{2,1},{3,4},{4,3},{5,6},{6,5},{7,0},{0,7},{9,10},{10,9},{11,... | collective-permute-start | bytes 516104 | tf_op jit(solution)/shard_map/ppermute | solution.py:555
  116.0 3.3 %copy-start.4 = (f32[42,8,128]{2,1,0:T(8,128)}, f32[42,8,128]{2,1,0:T(8,128)S(1)}, u32[]{:S(2)}) copy-start(f32[42,8,128]{2,1,0:T(8,128)S(1)} %collective-permute-done.67.z_even) | copy-start | bytes 516100
  119.3 0.7 copy-start.5
